TPU v7x, 32 devices: a whole 2x2x4 slice. The times are simulated.
32 devices in a mesh: row: 4 (over y, x), col: 8 (over z, core).
Axes of the slice: x: 2, y: 2, z: 4, core: 2. Of those that a mesh axis runs over, the one named last changes fastest.
Arguments:
- xblocks: bfloat16 [56, 8, 128, 128], P('row', 'col'), may hold values from -2 to 2
- xcols: int32 [56, 8], P('row', 'col'), may hold values from 0 to 6, as said below
- outcols: int32 [56, 16], P('row', 'col'), may hold values from 0 to 6, as said below
Outputs:
- square_blocks: bfloat16 [56, 16, 128, 128], P('row', 'col')
Inputs may be any that keep to these rules, and one draw needn't show every extreme that they name: xcols[m, t] is a block column within column tile t; over all block rows, the entries of one column tile take at most 3 distinct values. `outcols`: each entry names a block column of its column tile at which at least one block product of the window for that block row lands; entries of one row and tile may repeat.
All inputs are finite; a program needn't handle non-finite values.
Results may differ from a plain program's by a relative error of at most 0.001.
Values may be sent and summed in bfloat16 or wider, within the bound.
A program may use at most 64 MiB of HBM per device.

v0:
```python
import jax
import jax.numpy as jnp
from jax import lax
from jax.sharding import PartitionSpec as P

STEPS = 4


def passed_along(value, axis, steps):
    count = lax.axis_size(axis)
    pairs = [(source, (source + steps) % count) for source in range(count)]
    return lax.ppermute(value, axis, pairs)


def broadcast(value, axis, source):
    kept = jnp.where(lax.axis_index(axis) == source, value, 0).astype(value.dtype)
    return lax.psum(kept, axis)


def add_products(total, a_blocks, a_cols, b_blocks, b_cols, targets, offset):
    index = offset + a_cols
    chosen = jnp.take(b_blocks, index, axis=0)
    landing = jnp.take(b_cols, index, axis=0)
    product = jnp.einsum("mab,mbc->mac", a_blocks, chosen, preferred_element_type=jnp.float32)
    weight = (landing[:, None] == targets).astype(jnp.float32)
    return total + weight[:, :, None, None] * product[:, None]


def on_device(xblocks, xcols, outcols):
    row_count = lax.axis_size("row")
    col_count = lax.axis_size("col")
    per_panel = col_count // row_count
    block_rows = xblocks.shape[0]
    tile_cols = block_rows // per_panel
    block_size = xblocks.shape[2]
    kept = outcols.shape[1]
    row_here = lax.axis_index("row")
    own_blocks = xblocks[:, 0]
    own_cols = xcols[:, 0]
    total = jnp.zeros((block_rows, kept, block_size, block_size), jnp.float32)
    moving = (own_blocks, own_cols)
    for step_no in range(STEPS):
        panel = (row_here + step_no) % row_count
        if step_no > 0:
            moving = passed_along((moving[0], moving[1]), "row", -1)
        for half_no in range(per_panel):
            tile_blocks, tile_cols_ids = (
                broadcast(own_blocks, "col", per_panel * panel + half_no),
                broadcast(own_cols, "col", per_panel * panel + half_no),
            )
            total = add_products(
                total,
                tile_blocks,
                tile_cols_ids,
                moving[0],
                moving[1],
                outcols,
                half_no * tile_cols,
            )
    return total.astype(jnp.bfloat16)


def solution(mesh):
    in_specs = (P("row", "col", None, None), P("row", "col"), P("row", "col"))
    out_specs = P("row", "col", None, None)
    return jax.shard_map(
        on_device, mesh=mesh, in_specs=in_specs, out_specs=out_specs, check_vma=False
    )
```

profile of v0, /device:TPU:0, one launch (start us, length us, event | category | flops | bytes accessed | tf_op | source)
XLA Modules:
  0.0 120.9 jit_solution(17391470564263204695)
XLA Ops:
  6.5 3.9 %collective-permute-start.1 = (bf16[14,128,128]{2,1,0:T(8,128)(2,1)}, bf16[14,128,128]{2,1,0:T(8,128)(2,1)S(1)}, u32[]{:S(2)}, u32[]{:S(2)}) collective-permute-start(bf16[14,128,128]{2,1,0:T(8,128)(2,1)} %bitcast.29), channel_id=1, source_target_pairs={{0,24},{8,0},{16,8},{24,16},{1,25},{9,1},{17,9},{25,17},{2,26},{10... | collective-permute-start | bytes 1376264 | tf_op jit(solution)/shard_map/ppermute | solution.py:12
  10.4 0.5 collective-permute-start
  11.0 2.9 %broadcast_select_fusion.7 = (bf16[14,128,128]{2,1,0:T(8,128)(2,1)}, bf16[14,128,128]{2,1,0:T(8,128)(2,1)}, bf16[14,128,128]{2,1,0:T(8,128)(2,1)}, bf16[14,128,1...) fusion(pred[]{:T(512)S(6)} %eq.101, ...), kind=kLoop, calls=%fused_computation.48 | loop fusion | flops 1835008 | bytes 4128776 | tf_op jit(solution)/shard_map/jit(_where)/select_n | solution.py:16
  13.9 0.6 copy-done
  14.5 9.4 %all-reduce = (s32[14]{0:T(128)S(1)}, s32[14]{0:T(128)S(1)}, s32[14]{0:T(128)S(1)}, s32[14]{0:T(128)S(1)}, s32[14]{0:T(128)S(1)}, /*index=5*/s32[14]{0:T(128)S(1)}, s32[14]{0:T(128)S(1)}, s32[14]{0:T(128)S(1)}) all-reduce(s32[14]{0:T(128)S(1)} %get-tuple-element.62, ...), channel_id=1, replica_groups=mesh['row'=4,'col'=8] {'col'}, use_global_device_ids=true, to_apply=%region_14.17 | all-reduce | flops 112 | bytes 896 | tf_op jit(solution)/shard_map/psum | solution.py:17
  24.2 0.7 gather_fusion.2
  24.9 0.6 gather_fusion.3
  25.5 0.7 gather_fusion
  26.2 0.6 gather_fusion.1
  26.8 1.5 %collective-permute-start.2 = (s32[14]{0:T(128)S(1)}, s32[14]{0:T(128)S(1)}, u32[]{:S(2)}, u32[]{:S(2)}) collective-permute-start(s32[14]{0:T(128)S(1)} %collective-permute-done), channel_id=1, source_target_pairs={{0,24},{8,0},{16,8},{24,16},{1,25},{9,1},{17,9},{25,17},{2,26},{10... | collective-permute-start | bytes 176 | tf_op jit(solution)/shard_map/ppermute | solution.py:12
  28.3 0.7 gather_fusion.6
  29.0 0.7 gather_fusion.4
  29.7 0.6 collective-permute-start.3
  30.2 0.2 collective-permute-done.2
  30.4 2.4 %collective-permute-start.4 = (s32[14]{0:T(128)S(1)}, s32[14]{0:T(128)S(1)}, u32[]{:S(2)}, u32[]{:S(2)}) collective-permute-start(s32[14]{0:T(128)S(1)} %collective-permute-done.2), channel_id=1, source_target_pairs={{0,24},{8,0},{16,8},{24,16},{1,25},{9,1},{17,9},{25,17},{2,26},{10... | collective-permute-start | bytes 176 | tf_op jit(solution)/shard_map/ppermute | solution.py:12
  32.8 0.7 gather_fusion.10
  33.4 0.7 gather_fusion.8
  34.1 6.3 %collective-permute-done.4 = s32[14]{0:T(128)S(1)} collective-permute-done((s32[14]{0:T(128)S(1)}, s32[14]{0:T(128)S(1)}, u32[]{:S(2)}, u32[]{:S(2)}) %collective-permute-start.4) | collective-permute-done | bytes 88 | tf_op jit(solution)/shard_map/ppermute | solution.py:12
  40.5 0.7 gather_fusion.14
  41.1 1.4 %collective-permute-start.5 = (bf16[14,128,128]{2,1,0:T(8,128)(2,1)S(1)}, bf16[14,128,128]{2,1,0:T(8,128)(2,1)S(1)}, u32[]{:S(2)}, u32[]{:S(2)}) collective-permute-start(bf16[14,128,128]{2,1,0:T(8,128)(2,1)S(1)} %collective-permute-done.3), channel_id=1, source_target_pairs={{0,24},{8,0},{16,8},{24,16},{1,25},{9,1},{17,9},{25,17},{2,26},{10... | collective-permute-start | bytes 1376264 | tf_op jit(solution)/shard_map/ppermute | solution.py:12
  42.6 0.7 gather_fusion.12
  43.3 0.1 copy.19
  43.4 0.1 copy.18
  43.4 0.1 copy.17
  44.0 0.6 gather_fusion.7
  44.7 0.6 gather_fusion.5
  45.3 1.4 %gather_fusion.11 = bf16[14,128,128]{2,1,0:T(8,128)(2,1)} fusion(bf16[14,128,128]{2,1,0:T(8,128)(2,1)S(1)} %collective-permute-done.3, s32[1024]{0:T(1024)S(1)} %pad_clamp_fusion.2), kind=kCustom, calls=%fused_computation.13.clone | custom fusion | bytes 917560 | tf_op jit(solution)/shard_map/jit(_take)/gather | solution.py:22
  46.7 0.6 gather_fusion.9
  47.3 3.6 %collective-permute-done.5 = bf16[14,128,128]{2,1,0:T(8,128)(2,1)S(1)} collective-permute-done((bf16[14,128,128]{2,1,0:T(8,128)(2,1)S(1)}, bf16[14,128,128]{2,1,0:T(8,128)(2,1)S(1)}, u32[]{:S(2)}, u32[]{:S(2)}) %collective-permute-start.5) | collective-permute-done | bytes 458784 | tf_op jit(solution)/shard_map/ppermute | solution.py:12
  50.9 1.4 %gather_fusion.15 = bf16[14,128,128]{2,1,0:T(8,128)(2,1)} fusion(bf16[14,128,128]{2,1,0:T(8,128)(2,1)S(1)} %collective-permute-done.5, s32[1024]{0:T(1024)S(1)} %pad_clamp_fusion), kind=kCustom, calls=%fused_computation.15.clone | custom fusion | bytes 917560 | tf_op jit(solution)/shard_map/jit(_take)/gather | solution.py:22
  52.3 0.6 gather_fusion.13
  53.0 50.6 %all-reduce.4.cloned.1.call-done = (bf16[14,128,128]{2,1,0:T(8,128)(2,1)}, bf16[14,128,128]{2,1,0:T(8,128)(2,1)}, bf16[14,128,128]{2,1,0:T(8,128)(2,1)}, bf16[14...) async-done(((bf16[14,128,128]{2,1,0:T(8,128)(2,1)}, ...) | async-done | bytes 3670032 | tf_op jit(solution)/shard_map/psum | solution.py:17
  103.6 1.6 %fusion = f32[14,128,128]{2,1,0:T(8,128)S(1)} fusion(bf16[14,128,128]{2,1,0:T(8,128)(2,1)} %get-tuple-element.15, bf16[14,128,128]{2,1,0:T(8,128)(2,1)} %gather_fusion.15, pred[14]{0:T(512)(128)(4,1)S(1)} %get-tuple-element.37), kind=kOutput, calls=%fused_computation.17 | convolution fusion | flops 58949632 | bytes 1835022 | tf_op jit(solution)/shard_map/mab,mbc->mac/dot_general | solution.py:24
  105.2 0.4 fusion.2
  105.5 0.6 copy-done.2
  106.2 0.1 copy-done.8
  106.3 0.4 fusion.4
  106.7 0.7 copy-done.7
  107.3 0.4 fusion.6
  107.7 0.7 copy-done.6
  108.4 0.4 fusion.8
  108.7 0.7 copy-done.5
  109.4 0.4 fusion.10
  109.7 0.7 copy-done.4
  110.4 0.4 fusion.12
  110.8 0.7 copy-done.3
  111.4 0.4 fusion.14
  111.8 2.3 %add_convert_fusion = bf16[14,2,128,128]{3,2,1,0:T(8,128)(2,1)} fusion(f32[14,128,128]{2,1,0:T(8,128)S(1)} %fusion, f32[14,2]{1,0:T(8,128)S(1)} %copy.19, f32[14,128,128]{2,1,0:T(8,128)S(1)} %fusion.2, f32[14,2]{1,0:T(8,128)S(1)} %copy.18, f32[14,128,128]{2,1,0:T(8,128)S(1)} %fusion.4, f32[14,2]{1,0:T(8,128)S(1)} %copy.17, f32[14,128,128]{2,1,0:T(8,128)S(1)} %fusion.6, ...), kind=kLoop, calls=%fused_computation.16 | loop fusion | flops 7340032 | bytes 8258432 | tf_op jit(solution)/shard_map/convert_element_type | solution.py:60
  (50 shorter events, 0.7 us)
Async XLA Ops:
  6.5 97.0 %all-reduce.4.cloned.1.call-start = ((), (), s32[]{:S(2)}) async-start(), calls=%async_computation | async-start | bytes 7340032 | tf_op jit(solution)/shard_map/psum | solution.py:17
  6.5 23.1 %collective-permute-start.1 = (bf16[14,128,128]{2,1,0:T(8,128)(2,1)}, bf16[14,128,128]{2,1,0:T(8,128)(2,1)S(1)}, u32[]{:S(2)}, u32[]{:S(2)}) collective-permute-start(bf16[14,128,128]{2,1,0:T(8,128)(2,1)} %bitcast.29), channel_id=1, source_target_pairs={{0,24},{8,0},{16,8},{24,16},{1,25},{9,1},{17,9},{25,17},{2,26},{10... | collective-permute-start | bytes 1376264 | tf_op jit(solution)/shard_map/ppermute | solution.py:12
  10.4 16.4 %collective-permute-start = (s32[14]{0:T(128)}, s32[14]{0:T(128)S(1)}, u32[]{:S(2)}, u32[]{:S(2)}) collective-permute-start(s32[14]{0:T(128)} %bitcast.26), channel_id=1, source_target_pairs={{0,24},{8,0},{16,8},{24,16},{1,25},{9,1},{17,9},{25,17},{2,26},{10... | collective-permute-start | bytes 176 | tf_op jit(solution)/shard_map/ppermute | solution.py:12
  13.9 0.7 copy-start
  14.5 10.3 %copy-start.1 = (bf16[14,1,128,128]{3,2,1,0:T(8,128)(2,1)S(1)}, bf16[14,1,128,128]{3,2,1,0:T(8,128)(2,1)}, u32[]{:S(2)}) copy-start(bf16[14,1,128,128]{3,2,1,0:T(8,128)(2,1)} %param.7) | copy-start | bytes 1376260
  26.8 3.6 %collective-permute-start.2 = (s32[14]{0:T(128)S(1)}, s32[14]{0:T(128)S(1)}, u32[]{:S(2)}, u32[]{:S(2)}) collective-permute-start(s32[14]{0:T(128)S(1)} %collective-permute-done), channel_id=1, source_target_pairs={{0,24},{8,0},{16,8},{24,16},{1,25},{9,1},{17,9},{25,17},{2,26},{10... | collective-permute-start | bytes 176 | tf_op jit(solution)/shard_map/ppermute | solution.py:12
  29.7 11.4 %collective-permute-start.3 = (bf16[14,128,128]{2,1,0:T(8,128)(2,1)S(1)}, bf16[14,128,128]{2,1,0:T(8,128)(2,1)S(1)}, u32[]{:S(2)}, u32[]{:S(2)}) collective-permute-start(bf16[14,128,128]{2,1,0:T(8,128)(2,1)S(1)} %collective-permute-done.1), channel_id=1, source_target_pairs={{0,24},{8,0},{16,8},{24,16},{1,25},{9,1},{17,9},{25,17},{2,26},{10... | collective-permute-start | bytes 1376264 | tf_op jit(solution)/shard_map/ppermute | solution.py:12
  30.4 10.0 %collective-permute-start.4 = (s32[14]{0:T(128)S(1)}, s32[14]{0:T(128)S(1)}, u32[]{:S(2)}, u32[]{:S(2)}) collective-permute-start(s32[14]{0:T(128)S(1)} %collective-permute-done.2), channel_id=1, source_target_pairs={{0,24},{8,0},{16,8},{24,16},{1,25},{9,1},{17,9},{25,17},{2,26},{10... | collective-permute-start | bytes 176 | tf_op jit(solution)/shard_map/ppermute | solution.py:12
  33.4 9.8 %copy-start.10 = (s32[14,2]{0,1:T(2,128)S(1)}, s32[14,2]{0,1:T(2,128)}, u32[]{:S(2)}) copy-start(s32[14,2]{0,1:T(2,128)} %param.9) | copy-start | bytes 340
  41.1 9.8 %collective-permute-start.5 = (bf16[14,128,128]{2,1,0:T(8,128)(2,1)S(1)}, bf16[14,128,128]{2,1,0:T(8,128)(2,1)S(1)}, u32[]{:S(2)}, u32[]{:S(2)}) collective-permute-start(bf16[14,128,128]{2,1,0:T(8,128)(2,1)S(1)} %collective-permute-done.3), channel_id=1, source_target_pairs={{0,24},{8,0},{16,8},{24,16},{1,25},{9,1},{17,9},{25,17},{2,26},{10... | collective-permute-start | bytes 1376264 | tf_op jit(solution)/shard_map/ppermute | solution.py:12
  103.6 1.6 %copy-start.9 = (bf16[14,128,128]{2,1,0:T(8,128)(2,1)S(1)}, bf16[14,128,128]{2,1,0:T(8,128)(2,1)}, u32[]{:S(2)}) copy-start(bf16[14,128,128]{2,1,0:T(8,128)(2,1)} %get-tuple-element.16) | copy-start | bytes 1376260
  105.2 1.0 copy-start.2
  105.2 1.1 copy-start.8
  106.3 1.0 copy-start.7
  107.3 1.0 copy-start.6
  108.4 1.0 copy-start.5
  109.4 1.0 copy-start.4
  110.4 1.0 copy-start.3
Sparse Core Ops, SparseCore 0:
  14.0 89.5 all-reduce.3
where the time goes:
time: 121 us
  waiting for transfers between devices  60.8 us (50%)
  local copies, waits for them, and re-layouts  17.3 us (14%)
  between operations  13.7 us (11%)
  starting transfers between devices  10.3 us (9%)
  blocking collectives  9.43 us (8%)
  other arithmetic  5.35 us (4%)
  matrix products  4.04 us (3%)
    psum x1, waiting for transfers between devices, broadcast(): return lax.psum(kept, axis)  50.6 us
    ppermute x6, starting transfers between devices, passed_along(): return lax.ppermute(value, axis, pairs)  10.3 us
    ppermute x6, waiting for transfers between devices, passed_along(): return lax.ppermute(value, axis, pairs)  10.1 us
    psum x1, blocking collectives, broadcast(): return lax.psum(kept, axis)  9.43 us
    gather x8, local copies, waits for them, and re-layouts, add_products(): chosen = jnp.take(b_blocks, index, axis=0)  6.57 us
    gather x8, local copies, waits for them, and re-layouts, add_products(): landing = jnp.take(b_cols, index, axis=0)  5.26 us
    unnamed x22, local copies, waits for them, and re-layouts  4.7 us
    dot_general x8, matrix products, add_products(): jnp.einsum('mab,mbc->mac', a_blocks, chosen, preferred_element_type=jnp.f...  4.04 us
  transfers between devices with their start and end apart: 7, of which 4 were waited for; matrix products, arithmetic and copies ran while one was open for 13% of the time, Pallas kernels for 0%

commit v1 on v0

--- a/solution.py
+++ b/solution.py
@@ -14,7 +14,12 @@
 
 def broadcast(value, axis, source):
     kept = jnp.where(lax.axis_index(axis) == source, value, 0).astype(value.dtype)
-    return lax.psum(kept, axis)
+
+    def direct_bench(v0):
+        aux = lax.all_gather(v0, axis)
+        return jnp.sum(aux, axis=0)
+
+    return direct_bench(kept)
 
 
 def add_products(total, a_blocks, a_cols, b_blocks, b_cols, targets, offset):

time: 121 us -> 373 us (3.08)
  waiting for transfers between devices: 60.8 us -> 286 us
  other arithmetic: 5.35 us -> 34.3 us
    all_gather x0 -> x8, waiting for transfers between devices: none -> 270 us  [direct_bench(): aux = lax.all_gather(v0, axis)]
    psum x1 -> x0, waiting for transfers between devices: 50.6 us -> none  [broadcast(): return lax.psum(kept, axis)]
    reduce_sum x0 -> x16, other arithmetic: none -> 28.3 us  [direct_bench(): return jnp.sum(aux, axis=0)]
    psum x1 -> x0, blocking collectives: 9.43 us -> none  [broadcast(): return lax.psum(kept, axis)]
    unnamed x0 -> x1, blocking collectives: none -> 9.39 us
  transfers between devices with their start and end apart: 7 -> 14, of which waited for: 4 -> 10; matrix products, arithmetic and copies ran while one was open for 13% -> 11% of each run, Pallas kernels for 0% -> 0%
where the time goes in v1:
time: 373 us
  waiting for transfers between devices  286 us (77%)
  other arithmetic  34.3 us (9%)
  local copies, waits for them, and re-layouts  15.2 us (4%)
  between operations  14.5 us (4%)
  starting transfers between devices  10.8 us (3%)
  blocking collectives  9.39 us (3%)
    all_gather x8, waiting for transfers between devices, direct_bench(): aux = lax.all_gather(v0, axis)  270 us
    reduce_sum x16, other arithmetic, direct_bench(): return jnp.sum(aux, axis=0)  28.3 us
    ppermute x6, waiting for transfers between devices, passed_along(): return lax.ppermute(value, axis, pairs)  11.7 us
    ppermute x6, starting transfers between devices, passed_along(): return lax.ppermute(value, axis, pairs)  10.5 us
    unnamed x1, blocking collectives  9.39 us
  transfers between devices with their start and end apart: 14, of which 10 were waited for; matrix products, arithmetic and copies ran while one was open for 11% of the time, Pallas kernels for 0%

profile of v1, /device:TPU:0, one launch (start us, length us, event | category | flops | bytes accessed | tf_op | source)
XLA Modules:
  0.0 372.9 jit_solution(15612006045439190873)
XLA Ops:
  6.5 2.9 broadcast_select_fusion.7
  9.5 0.7 all-gather.33.cloned.1.call-update
  10.3 0.7 all-gather.35.cloned.1.call-update
  11.6 0.5 all-gather.29.cloned.1.call-update
  12.7 0.7 all-gather.25.cloned.1.call-update
  13.5 3.9 %collective-permute-start.1 = (bf16[14,128,128]{2,1,0:T(8,128)(2,1)S(1)}, bf16[14,128,128]{2,1,0:T(8,128)(2,1)S(1)}, u32[]{:S(2)}, u32[]{:S(2)}) collective-permute-start(bf16[14,128,128]{2,1,0:T(8,128)(2,1)S(1)} %bitcast.70), channel_id=1, source_target_pairs={{0,24},{8,0},{16,8},{24,16},{1,25},{9,1},{17,9},{25,17},{2,26},{10... | collective-permute-start | bytes 1376264 | tf_op jit(solution)/shard_map/ppermute | solution.py:12
  17.5 0.5 collective-permute-start
  18.0 0.6 dynamic-slice
  19.9 9.4 %all-reduce.8 = (s32[112]{0:T(128)S(1)}, s32[112]{0:T(128)S(1)}, s32[112]{0:T(128)S(1)}, s32[112]{0:T(128)S(1)}, s32[112]{0:T(128)S(1)}, /*index=5*/s32[112]{0:T(128)S(1)}, s32[112]{0:T(128)S(1)}, s32[112]{0:T(128)S(1)}) all-reduce(s32[112]{0:T(128)S(1)} %fusion.47, s32[112]{0:T(128)S(1)} %fusion.45, ...), channel_id=16, replica_groups=mesh['row'=4,'col'=8] {'col'}, use_global_device_ids=true, to_apply=%add.7 | all-reduce | flops 896 | bytes 7168
  30.0 0.7 gather_fusion.2
  31.0 0.6 gather_fusion.1
  31.7 0.7 gather_fusion
  32.3 0.6 gather_fusion.3
  33.0 1.5 collective-permute-start.2
  34.5 0.7 gather_fusion.4
  35.1 0.7 gather_fusion.6
  35.8 0.6 collective-permute-start.3
  36.6 2.3 collective-permute-start.4
  38.9 0.7 gather_fusion.8
  39.6 0.7 gather_fusion.10
  40.3 6.7 %collective-permute-done.4 = s32[14]{0:T(128)S(1)} collective-permute-done((s32[14]{0:T(128)S(1)}, s32[14]{0:T(128)S(1)}, u32[]{:S(2)}, u32[]{:S(2)}) %collective-permute-start.4) | collective-permute-done | bytes 88 | tf_op jit(solution)/shard_map/ppermute | solution.py:12
  46.9 0.7 gather_fusion.14
  47.6 1.7 collective-permute-start.5
  49.3 0.7 gather_fusion.12
  50.7 0.6 gather_fusion.5
  51.4 0.6 gather_fusion.7
  52.0 1.4 gather_fusion.9
  53.4 0.6 gather_fusion.11
  54.0 4.8 %collective-permute-done.5 = bf16[14,128,128]{2,1,0:T(8,128)(2,1)S(1)} collective-permute-done((bf16[14,128,128]{2,1,0:T(8,128)(2,1)S(1)}, bf16[14,128,128]{2,1,0:T(8,128)(2,1)S(1)}, u32[]{:S(2)}, u32[]{:S(2)}) %collective-permute-start.5) | collective-permute-done | bytes 458784 | tf_op jit(solution)/shard_map/ppermute | solution.py:12
  58.9 1.4 gather_fusion.13
  60.2 0.6 gather_fusion.15
  60.9 3.8 %bitcast_reduce_fusion.1 = bf16[14,128,128]{2,1,0:T(8,128)(2,1)} fusion(bf16[8,14,128,128]{3,2,1,0:T(8,128)(2,1)} %bitcast.73), kind=kLoop, calls=%fused_computation.17 | loop fusion | flops 1605632 | bytes 4128768 | tf_op jit(solution)/shard_map/reduce_sum | solution.py:20
  64.7 33.5 %all-gather.33.cloned.1.call-done = bf16[112,1,128,128]{3,2,1,0:T(8,128)(2,1)} async-done(((bf16[14,1,128,128]{3,2,1,0:T(8,128)(2,1)}), bf16[112,1,128,128]{3,2,1,0:T(8,128)(2,1)}) %all-gather.33.cloned.1.call-update) | async-done | bytes 3670032 | tf_op jit(solution)/shard_map/all_gather | solution.py:19
  98.2 3.6 bitcast_reduce_fusion.3
  101.8 39.6 %all-gather.35.cloned.1.call-done = bf16[112,1,128,128]{3,2,1,0:T(8,128)(2,1)} async-done(((bf16[14,1,128,128]{3,2,1,0:T(8,128)(2,1)}), bf16[112,1,128,128]{3,2,1,0:T(8,128)(2,1)}) %all-gather.35.cloned.1.call-update) | async-done | bytes 3670032 | tf_op jit(solution)/shard_map/all_gather | solution.py:19
  141.4 3.6 bitcast_reduce_fusion.2
  145.0 39.4 %all-gather.39.cloned.1.call-done = bf16[112,1,128,128]{3,2,1,0:T(8,128)(2,1)} async-done(((bf16[14,1,128,128]{3,2,1,0:T(8,128)(2,1)}), bf16[112,1,128,128]{3,2,1,0:T(8,128)(2,1)}) %all-gather.39.cloned.1.call-update) | async-done | bytes 3670032 | tf_op jit(solution)/shard_map/all_gather | solution.py:19
  184.4 3.6 bitcast_reduce_fusion
  188.0 39.4 %all-gather.29.cloned.1.call-done = bf16[112,1,128,128]{3,2,1,0:T(8,128)(2,1)} async-done(((bf16[14,1,128,128]{3,2,1,0:T(8,128)(2,1)}), bf16[112,1,128,128]{3,2,1,0:T(8,128)(2,1)}) %all-gather.29.cloned.1.call-update) | async-done | bytes 3670032 | tf_op jit(solution)/shard_map/all_gather | solution.py:19
  227.3 3.6 bitcast_reduce_fusion.5
  230.9 39.4 %all-gather.31.cloned.1.call-done = bf16[112,1,128,128]{3,2,1,0:T(8,128)(2,1)} async-done(((bf16[14,1,128,128]{3,2,1,0:T(8,128)(2,1)}), bf16[112,1,128,128]{3,2,1,0:T(8,128)(2,1)}) %all-gather.31.cloned.1.call-update) | async-done | bytes 3670032 | tf_op jit(solution)/shard_map/all_gather | solution.py:19
  270.3 3.6 bitcast_reduce_fusion.4
  274.0 39.5 %all-gather.25.cloned.1.call-done = bf16[112,1,128,128]{3,2,1,0:T(8,128)(2,1)} async-done(((bf16[14,1,128,128]{3,2,1,0:T(8,128)(2,1)}), bf16[112,1,128,128]{3,2,1,0:T(8,128)(2,1)}) %all-gather.25.cloned.1.call-update) | async-done | bytes 3670032 | tf_op jit(solution)/shard_map/all_gather | solution.py:19
  313.5 3.6 bitcast_reduce_fusion.7
  317.1 39.6 %all-gather.27.cloned.1.call-done = bf16[112,1,128,128]{3,2,1,0:T(8,128)(2,1)} async-done(((bf16[14,1,128,128]{3,2,1,0:T(8,128)(2,1)}), bf16[112,1,128,128]{3,2,1,0:T(8,128)(2,1)}) %all-gather.27.cloned.1.call-update) | async-done | bytes 3670032 | tf_op jit(solution)/shard_map/all_gather | solution.py:19
  356.6 2.7 bitcast_reduce_fusion.6
  359.8 0.6 copy-done.2
  363.7 2.3 add_convert_fusion
  (115 shorter events, 7.7 us)
Async XLA Ops:
  6.5 54.4 %all-gather.37.cloned.1.call-start = ((), (), s32[]{:S(2)}) async-start(), calls=%async_computation.6 | async-start | bytes 4128768 | tf_op jit(solution)/shard_map/all_gather | solution.py:19
  9.4 4.1 %copy-start.1 = (bf16[14,1,128,128]{3,2,1,0:T(8,128)(2,1)S(1)}, bf16[14,1,128,128]{3,2,1,0:T(8,128)(2,1)}, u32[]{:S(2)}) copy-start(bf16[14,1,128,128]{3,2,1,0:T(8,128)(2,1)} %param.7) | copy-start | bytes 1376260
  9.4 8.0 %copy-start = (s32[14,1]{0,1:T(1,128)S(1)}, s32[14,1]{0,1:T(1,128)}, u32[]{:S(2)}) copy-start(s32[14,1]{0,1:T(1,128)} %param.8) | copy-start | bytes 172
  9.4 8.6 %copy-start.12 = (u32[32]{0:T(128)S(1)}, u32[32]{0:T(128)}, u32[]{:S(2)}) copy-start(u32[32]{0:T(128)} %constant.77) | copy-start | bytes 388
  9.5 88.7 %all-gather.33.cloned.1.call-start = ((), (), s32[]{:S(2)}) async-start(), calls=%async_computation.4 | async-start | bytes 4128768 | tf_op jit(solution)/shard_map/all_gather | solution.py:19
  10.2 131.1 %all-gather.35.cloned.1.call-start = ((), (), s32[]{:S(2)}) async-start(), calls=%async_computation.5 | async-start | bytes 4128768 | tf_op jit(solution)/shard_map/all_gather | solution.py:19
  11.0 173.4 %all-gather.39.cloned.1.call-start = ((), (), s32[]{:S(2)}) async-start(), calls=%async_computation.7 | async-start | bytes 4128768 | tf_op jit(solution)/shard_map/all_gather | solution.py:19
  11.5 215.8 %all-gather.29.cloned.1.call-start = ((), (), s32[]{:S(2)}) async-start(), calls=%async_computation.2 | async-start | bytes 4128768 | tf_op jit(solution)/shard_map/all_gather | solution.py:19
  12.1 258.2 %all-gather.31.cloned.1.call-start = ((), (), s32[]{:S(2)}) async-start(), calls=%async_computation.3 | async-start | bytes 4128768 | tf_op jit(solution)/shard_map/all_gather | solution.py:19
  12.7 300.8 %all-gather.25.cloned.1.call-start = ((), (), s32[]{:S(2)}) async-start(), calls=%async_computation | async-start | bytes 4128768 | tf_op jit(solution)/shard_map/all_gather | solution.py:19
  13.4 343.2 %all-gather.27.cloned.1.call-start = ((), (), s32[]{:S(2)}) async-start(), calls=%async_computation.1 | async-start | bytes 4128768 | tf_op jit(solution)/shard_map/all_gather | solution.py:19
  13.5 22.3 %collective-permute-start.1 = (bf16[14,128,128]{2,1,0:T(8,128)(2,1)S(1)}, bf16[14,128,128]{2,1,0:T(8,128)(2,1)S(1)}, u32[]{:S(2)}, u32[]{:S(2)}) collective-permute-start(bf16[14,128,128]{2,1,0:T(8,128)(2,1)S(1)} %bitcast.70), channel_id=1, source_target_pairs={{0,24},{8,0},{16,8},{24,16},{1,25},{9,1},{17,9},{25,17},{2,26},{10... | collective-permute-start | bytes 1376264 | tf_op jit(solution)/shard_map/ppermute | solution.py:12
  17.5 15.5 %collective-permute-start = (s32[14]{0:T(128)S(1)}, s32[14]{0:T(128)S(1)}, u32[]{:S(2)}, u32[]{:S(2)}) collective-permute-start(s32[14]{0:T(128)S(1)} %bitcast.67), channel_id=1, source_target_pairs={{0,24},{8,0},{16,8},{24,16},{1,25},{9,1},{17,9},{25,17},{2,26},{10... | collective-permute-start | bytes 176 | tf_op jit(solution)/shard_map/ppermute | solution.py:12
  32.3 17.6 %copy-start.11 = (s32[14,2]{0,1:T(2,128)S(1)}, s32[14,2]{0,1:T(2,128)}, u32[]{:S(2)}) copy-start(s32[14,2]{0,1:T(2,128)} %param.9) | copy-start | bytes 340
  33.0 3.6 collective-permute-start.2
  35.8 11.8 %collective-permute-start.3 = (bf16[14,128,128]{2,1,0:T(8,128)(2,1)S(1)}, bf16[14,128,128]{2,1,0:T(8,128)(2,1)S(1)}, u32[]{:S(2)}, u32[]{:S(2)}) collective-permute-start(bf16[14,128,128]{2,1,0:T(8,128)(2,1)S(1)} %collective-permute-done.1), channel_id=1, source_target_pairs={{0,24},{8,0},{16,8},{24,16},{1,25},{9,1},{17,9},{25,17},{2,26},{10... | collective-permute-start | bytes 1376264 | tf_op jit(solution)/shard_map/ppermute | solution.py:12
  36.6 10.3 %collective-permute-start.4 = (s32[14]{0:T(128)S(1)}, s32[14]{0:T(128)S(1)}, u32[]{:S(2)}, u32[]{:S(2)}) collective-permute-start(s32[14]{0:T(128)S(1)} %collective-permute-done.2), channel_id=1, source_target_pairs={{0,24},{8,0},{16,8},{24,16},{1,25},{9,1},{17,9},{25,17},{2,26},{10... | collective-permute-start | bytes 176 | tf_op jit(solution)/shard_map/ppermute | solution.py:12
  47.6 11.3 %collective-permute-start.5 = (bf16[14,128,128]{2,1,0:T(8,128)(2,1)S(1)}, bf16[14,128,128]{2,1,0:T(8,128)(2,1)S(1)}, u32[]{:S(2)}, u32[]{:S(2)}) collective-permute-start(bf16[14,128,128]{2,1,0:T(8,128)(2,1)S(1)} %collective-permute-done.3), channel_id=1, source_target_pairs={{0,24},{8,0},{16,8},{24,16},{1,25},{9,1},{17,9},{25,17},{2,26},{10... | collective-permute-start | bytes 1376264 | tf_op jit(solution)/shard_map/ppermute | solution.py:12
  356.6 2.8 copy-start.3
  356.6 2.8 copy-start.4
  359.4 1.0 copy-start.2
  359.4 1.1 copy-start.5
  359.4 1.5 copy-start.6
  360.5 1.1 copy-start.7
  360.9 1.1 copy-start.8
  361.6 1.1 copy-start.9
  362.0 1.1 copy-start.10
Sparse Core Ops, SparseCore 0:
  9.6 45.4 all-gather.36
  56.7 41.4 all-gather.32
  99.9 41.4 all-gather.34
  142.9 41.4 all-gather.38
  185.8 41.4 all-gather.28
  228.8 41.4 all-gather.30
  272.0 41.4 all-gather.24
  315.1 41.4 all-gather.26
